TPU v7x, 512 devices: a whole 4x8x8 slice. The times are simulated.
512 devices in a mesh: item: 8 (over y), rows: 32 (over z, x_hi, core), hid: 2 (over x_lo).
Axes of the slice: x: 4 (x_hi: 2, x_lo: 2; x = x_hi * 2 + x_lo), y: 8, z: 8, core: 2. Of those that a mesh axis runs over, the one named last changes fastest.
Arguments:
- latents: float32 [16, 32, 2048], P('item', 'rows'), may hold values from -6 to 6
- heights: int32 [16], P('item'), may hold values from 8 to 32, as said below
- widths: int32 [16], P('item'), may hold values from 8 to 32, as said below
- slot_item: int32 [16], P('item'), may hold values from 0 to 15, each once
- step_index: int32 [1], replicated, may hold values from 0 to 27
- cond_table: float32 [16, 5, 1536], replicated, may hold values from -9 to 9
- text_kv: bfloat16 [16, 2, 154, 768], P('item', None, None, 'hid'), may hold values from -175 to 175
- patch_weight: bfloat16 [64, 1536], replicated, may hold values from -0.75 to 0.75
- qkv_weight: bfloat16 [3, 1536, 768], P(None, ('item', 'rows'), 'hid'), may hold values from -0.15625 to 0.15625
- out_weight: bfloat16 [768, 1536], P('hid', ('item', 'rows')), may hold values from -0.21875 to 0.21875
- final_weight: bfloat16 [1536, 64], replicated, may hold values from -0.15625 to 0.15625
Outputs:
- next_latents: float32 [16, 32, 2048], P('item', 'rows')
- denoised: float32 [16, 32, 2048], P('item', 'rows')
Inputs may be any that keep to these rules, and one draw needn't show every extreme that they name: `heights`: every grid has at least 8 rows, and some item has exactly 32. `widths`: every grid has at least 8 columns, and some item has exactly 32. `slot_item`: each request is served by exactly one slot.
All inputs are finite; a program needn't handle non-finite values.
Results may differ from a plain program's by a relative error of at most 0.007.
Values may be sent and summed in bfloat16 or wider, within the bound.
A program may use at most 64 MiB of HBM per device.

v0:
```python
import jax
import jax.numpy as jnp
from jax import lax
from jax.sharding import PartitionSpec as P

HD = 64
STEPS = 28


def sigma_level(position):
    fraction = 1.0 - position / STEPS
    return 3.0 * fraction / (1.0 + 2.0 * fraction)


def position_embed(row_pos, col_count, model_width):
    quarter = model_width // 4
    frequency = 1.0 / 10000.0 ** (jnp.arange(quarter, dtype=jnp.float32) / quarter)
    col_pos = jnp.arange(col_count, dtype=jnp.float32)
    row_angle = row_pos[:, None] * frequency[None, :]
    col_angle = col_pos[:, None] * frequency[None, :]
    row_part = jnp.concatenate([jnp.sin(row_angle), jnp.cos(row_angle)], 1)
    col_part = jnp.concatenate([jnp.sin(col_angle), jnp.cos(col_angle)], 1)
    row_full = jnp.broadcast_to(
        row_part[:, None, :], (row_pos.shape[0], col_count, model_width // 2)
    )
    col_full = col_part[None, :, :]
    return jnp.concatenate([row_full, col_full], 2)


def normalize(values):
    mean_rows = jnp.mean(values, -1, keepdims=True)
    centered = values - mean_rows
    return centered * lax.rsqrt(jnp.mean(centered * centered, -1, keepdims=True) + 1e-06)


def body(
    latents,
    heights,
    widths,
    slot_item,
    step_index,
    cond_table,
    text_kv,
    patch_weight,
    qkv_weight,
    out_weight,
    final_weight,
):
    slot_count = latents.shape[0]
    rows_here = latents.shape[1]
    channels = patch_weight.shape[0]
    model_width = patch_weight.shape[1]
    col_count = latents.shape[2] // channels
    local_width = text_kv.shape[3]
    heads_here = local_width // HD
    text_count = text_kv.shape[2]
    per_slot = rows_here * col_count
    tok_rows = slot_count * per_slot
    row_start = lax.axis_index("rows") * rows_here
    row_pos = (row_start + jnp.arange(rows_here, dtype=jnp.int32)).astype(jnp.float32)
    patches = latents.reshape(tok_rows, channels).astype(jnp.bfloat16)
    embedded = jnp.dot(patches, patch_weight, preferred_element_type=jnp.float32).reshape(
        slot_count, per_slot, model_width
    )
    embedded = embedded + position_embed(row_pos, col_count, model_width)
    entries = cond_table.shape[0]
    chosen = (slot_item[:, None] == jnp.arange(entries, dtype=jnp.int32)[None, :]).astype(
        jnp.float32
    )
    conditions = jnp.dot(
        chosen, cond_table.reshape(entries, 5 * model_width), precision=lax.Precision.HIGHEST
    )
    conditions = conditions.reshape(slot_count, 5, model_width)
    normed = (normalize(embedded) * (1.0 + conditions[:, 1:2, :]) + conditions[:, 0:1, :]).astype(
        jnp.bfloat16
    )
    flat_rows = normed.reshape(tok_rows, model_width)
    projected = jnp.einsum(
        "td,kdh->kth",
        flat_rows,
        lax.all_gather(qkv_weight, ("item", "rows"), axis=1, tiled=True),
        preferred_element_type=jnp.float32,
    )
    projected = projected.astype(jnp.bfloat16)
    queries = projected[0].reshape(slot_count, per_slot, heads_here, HD)
    image_kv = projected[1:].reshape(2, slot_count, rows_here, col_count, local_width)
    score_scale = HD ** (-0.5)
    text_keys = text_kv[:, 0].reshape(slot_count, text_count, heads_here, HD)
    text_vals = text_kv[:, 1].reshape(slot_count, text_count, heads_here, HD)
    text_score = (
        jnp.einsum("sqhd,skhd->shqk", queries, text_keys, preferred_element_type=jnp.float32)
        * score_scale
    )
    first_top = jnp.max(text_score, -1)
    text_weights = jnp.exp(text_score - first_top[..., None])
    first_total = jnp.sum(text_weights, -1)
    first_acc = jnp.einsum(
        "shqk,skhd->shqd",
        text_weights.astype(jnp.bfloat16),
        text_vals,
        preferred_element_type=jnp.float32,
    )
    col_live = jnp.arange(col_count, dtype=jnp.int32)[None, :] < widths[:, None]
    gathered = lax.all_gather(image_kv, "rows", axis=2, tiled=True)
    run_top = first_top
    run_total = first_total
    run_acc = first_acc
    key_rows = gathered.shape[2]
    key_piece = gathered[0].reshape(slot_count, key_rows * col_count, heads_here, HD)
    val_piece = gathered[1].reshape(slot_count, key_rows * col_count, heads_here, HD)
    scores = (
        jnp.einsum("sqhd,skhd->shqk", queries, key_piece, preferred_element_type=jnp.float32)
        * score_scale
    )
    key_index = jnp.arange(key_rows, dtype=jnp.int32)
    live_mask = (key_index[None, :, None] < heights[:, None, None]) & col_live[:, None, :]
    live_mask = live_mask.reshape(slot_count, 1, 1, key_rows * col_count)
    scores = jnp.where(live_mask, scores, -1e30)
    new_top = jnp.maximum(run_top, jnp.max(scores, -1))
    factor = jnp.exp(run_top - new_top)
    weights = jnp.exp(scores - new_top[..., None])
    run_total = run_total * factor + jnp.sum(weights, -1)
    run_acc = run_acc * factor[..., None] + jnp.einsum(
        "shqk,skhd->shqd",
        weights.astype(jnp.bfloat16),
        val_piece,
        preferred_element_type=jnp.float32,
    )
    run_top, run_total, run_acc = (new_top, run_total, run_acc)
    attended = (
        (run_acc / run_total[..., None])
        .transpose(0, 2, 1, 3)
        .reshape(tok_rows, local_width)
        .astype(jnp.bfloat16)
    )
    partial_value = jnp.dot(
        attended,
        lax.all_gather(out_weight, ("item", "rows"), axis=1, tiled=True),
        preferred_element_type=jnp.float32,
    )
    summed = lax.psum(partial_value.astype(jnp.bfloat16), "hid").astype(jnp.float32)
    summed = summed.reshape(slot_count, per_slot, model_width)
    residual = embedded + conditions[:, 2:3, :] * summed
    final_in = (normalize(residual) * (1.0 + conditions[:, 4:5, :]) + conditions[:, 3:4, :]).astype(
        jnp.bfloat16
    )
    velocity = jnp.dot(
        final_in.reshape(tok_rows, model_width), final_weight, preferred_element_type=jnp.float32
    )
    position = step_index[0].astype(jnp.float32)
    sigma_now = sigma_level(position)
    sigma_next = sigma_level(position + 1.0)
    row_global = row_start + jnp.arange(rows_here, dtype=jnp.int32)
    live_patch = (row_global[None, :, None] < heights[:, None, None]) & col_live[:, None, :]
    velocity = velocity.reshape(slot_count, rows_here, col_count, channels)
    live_velocity = jnp.where(live_patch[..., None], velocity, 0.0).reshape(
        slot_count, rows_here, col_count * channels
    )
    next_latents = latents + (sigma_next - sigma_now) * live_velocity
    denoised = latents - sigma_now * live_velocity
    return (next_latents, denoised)


def solution(mesh):
    return jax.shard_map(
        body,
        mesh=mesh,
        in_specs=(
            P("item", "rows", None),
            P("item"),
            P("item"),
            P("item"),
            P(),
            P(),
            P("item", None, None, "hid"),
            P(),
            P(None, ("item", "rows"), "hid"),
            P("hid", ("item", "rows")),
            P(),
        ),
        out_specs=(P("item", "rows", None), P("item", "rows", None)),
        check_vma=False,
    )
```

profile of v0, /device:TPU:1, one launch (start us, length us, event | category | flops | bytes accessed | tf_op | source)
XLA Modules:
  0.0 422.9 jit_solution(1402297968687768749)
XLA Ops:
  7.2 0.0 all-gather.5.cloned.1.call-start
  7.2 1.4 copy.35
  8.6 0.0 all-gather.5.cloned.1.call-update
  8.6 0.0 all-gather.9.cloned.1.call-start
  8.7 0.7 all-gather.9.cloned.1.call-update
  9.4 0.0 all-gather.7.cloned.1.call-start
  9.5 0.1 fusion.49
  9.5 0.2 fusion.42
  9.8 0.8 convert_reduce_fusion
  10.6 0.1 convert_element_type.46
  10.7 1.2 fusion.56
  11.9 0.2 multiply_reduce_fusion.1
  12.1 0.3 fusion.25
  12.4 0.1 add_convert_fusion.1
  12.6 136.8 %all-gather.5.cloned.1.call-done = bf16[3,1536,384]{2,0,1:T(4,128)(2,1)} async-done(((bf16[3,6,384]{2,0,1:T(4,128)(2,1)}), bf16[3,1536,384]{2,0,1:T(4,128)(2,1)}) %all-gather.5.cloned.1.call-update) | async-done | bytes 3538960 | tf_op jit(solution)/shard_map/all_gather | solution.py:81
  149.4 3.1 fusion.20
  152.5 0.6 slice.48
  153.1 0.0 all-gather.7.cloned.1.call-update
  153.2 0.0 all-reduce.2.cloned.1.call-start
  153.2 0.1 broadcast_and_fusion.1
  153.3 0.1 broadcast_and_fusion
  153.4 0.1 and.40
  153.5 0.7 fusion.54
  154.2 0.5 copy.37
  154.7 0.5 copy.39
  155.2 109.8 %all-gather.9.cloned.1.call-done = bf16[256,6,384]{2,1,0:T(8,128)(2,1)} async-done(((bf16[1,6,384]{2,1,0:T(8,128)(2,1)}), bf16[256,6,384]{2,1,0:T(8,128)(2,1)}) %all-gather.9.cloned.1.call-update) | async-done | bytes 1179664 | tf_op jit(solution)/shard_map/all_gather | solution.py:138
  265.0 3.3 reshape.279
  268.3 0.1 reshape_squeeze.15
  268.4 0.3 fusion.57
  268.7 0.2 fusion.28
  268.9 85.4 %all-gather.7.cloned.1.call-done = bf16[2,2,32,32,384]{4,3,2,1,0:T(8,128)(2,1)} async-done(((bf16[2,2,1,32,384]{4,3,2,1,0:T(8,128)(2,1)}), bf16[2,2,32,32,384]{4,3,2,1,0:T(8,128)(2,1)}) %all-gather.7.cloned.1.call-update) | async-done | bytes 3145744 | tf_op jit(solution)/shard_map/all_gather | solution.py:104
  354.4 3.5 fusion.53
  357.8 3.7 reshape_squeeze.18
  361.6 3.4 fusion.58
  365.0 5.9 %reshape_squeeze.19 = bf16[2,1024,6,64]{3,2,1,0:T(8,128)(2,1)} reshape(bf16[1,2,32,32,384]{4,3,2,1,0:T(8,128)(2,1)} %get-tuple-element.5) | data formatting | bytes 3145728 | tf_op jit(solution)/shard_map/reshape;squeeze | solution.py:110
  370.9 0.4 fusion.8
  371.3 3.3 fusion.16
  374.6 0.3 fusion.19
  375.0 0.1 convert_element_type.54
  375.1 0.7 copy-done.1
  375.9 1.2 convolution_convert_fusion
  377.8 34.3 %all-reduce.2.cloned.1.call-done = bf16[2,32,1536]{2,1,0:T(8,128)(2,1)} async-done(((bf16[2,32,1536]{2,1,0:T(8,128)(2,1)}), bf16[2,32,1536]{2,1,0:T(8,128)(2,1)}) %all-reduce.2.cloned.1.call-update) | async-done | bytes 196624 | tf_op jit(solution)/shard_map/psum | solution.py:141
  412.1 1.1 fusion.38
  413.2 1.1 multiply_reduce_fusion
  414.3 1.2 broadcast_multiply_fusion
  415.5 0.1 mul.213
  415.6 0.1 mul.214
  415.7 0.6 fusion.55
  (31 shorter events, 0.2 us)
Async XLA Ops:
  7.2 4.9 %copy-start = (f32[16,5,1536]{2,0,1:T(8,128)S(1)}, f32[16,5,1536]{2,0,1:T(8,128)}, u32[]{:S(2)}) copy-start(f32[16,5,1536]{2,0,1:T(8,128)} %param.16) | copy-start | bytes 1474564
  7.2 4.9 %copy-start.4 = (s32[2]{0:T(128)S(1)}, s32[2]{0:T(128)}, u32[]{:S(2)}) copy-start(s32[2]{0:T(128)} %param.14) | copy-start | bytes 28
  7.2 142.2 %all-gather.5.cloned.1.call-start = ((), (), s32[]{:S(2)}) async-start(), calls=%async_computation | async-start | bytes 4737024 | tf_op jit(solution)/shard_map/all_gather | solution.py:81
  8.6 256.3 %all-gather.9.cloned.1.call-start = ((), (), s32[]{:S(2)}) async-start(), calls=%async_computation.3 | async-start | bytes 1579008 | tf_op jit(solution)/shard_map/all_gather | solution.py:138
  9.4 345.0 %all-gather.7.cloned.1.call-start = ((), (), s32[]{:S(2)}) async-start(), calls=%async_computation.1 | async-start | bytes 3244032 | tf_op jit(solution)/shard_map/all_gather | solution.py:104
  149.4 3.9 copy-start.5
  149.4 3.9 copy-start.6
  149.4 4.1 copy-start.2
  153.2 258.9 %all-reduce.2.cloned.1.call-start = ((), (), s32[]{:S(2)}) async-start(), calls=%async_computation.2 | async-start | bytes 393216 | tf_op jit(solution)/shard_map/psum | solution.py:141
  374.6 1.3 copy-start.1
  375.0 39.3 %copy-start.7 = (bf16[1536,64]{0,1:T(8,128)(2,1)S(1)}, bf16[1536,64]{0,1:T(8,128)(2,1)}, u32[]{:S(2)}) copy-start(bf16[1536,64]{0,1:T(8,128)(2,1)} %param.21) | copy-start | bytes 589828
  377.0 38.7 %copy-start.3 = (f32[2,1,2048]{2,1,0:T(1,128)S(1)}, f32[2,1,2048]{2,1,0:T(1,128)}, u32[]{:S(2)}) copy-start(f32[2,1,2048]{2,1,0:T(1,128)} %param.11) | copy-start | bytes 49156
Sparse Core Ops, SparseCore 0:
  12.5 136.7 all-gather.4
  153.5 111.3 all-gather.8
  268.3 86.0 all-gather.6
  377.2 34.8 all-reduce.1
where the time goes:
time: 423 us
  waiting for transfers between devices  367 us (87%)
  local copies, waits for them, and re-layouts  21.5 us (5%)
  between operations  14.8 us (3%)
  matrix products  14.3 us (3%)
  other arithmetic  5.08 us (1%)
    all_gather x1, waiting for transfers between devices, body(): lax.all_gather(qkv_weight, ('item', 'rows'), axis=1, tiled=True)  137 us
    all_gather x1, waiting for transfers between devices, body(): lax.all_gather(out_weight, ('item', 'rows'), axis=1, tiled=True)  110 us
    all_gather x1, waiting for transfers between devices, body(): gathered = lax.all_gather(image_kv, 'rows', axis=2, tiled=True)  85.4 us
    psum x1, waiting for transfers between devices, body(): lax.psum(partial_value.astype(jnp.bfloat16), 'hid').astype(jnp.float32)  34.3 us
  transfers between devices with their start and end apart: 4, of which 4 were waited for; matrix products, arithmetic and copies ran while one was open for 3% of the time, Pallas kernels for 0%

commit v1 on v0

--- a/solution.py
+++ b/solution.py
@@ -138,7 +138,9 @@
         lax.all_gather(out_weight, ("item", "rows"), axis=1, tiled=True),
         preferred_element_type=jnp.float32,
     )
-    summed = lax.psum(partial_value.astype(jnp.bfloat16), "hid").astype(jnp.float32)
+    summed = jnp.sum(lax.all_gather(partial_value.astype(jnp.bfloat16), "hid"), axis=0).astype(
+        jnp.float32
+    )
     summed = summed.reshape(slot_count, per_slot, model_width)
     residual = embedded + conditions[:, 2:3, :] * summed
     final_in = (normalize(residual) * (1.0 + conditions[:, 4:5, :]) + conditions[:, 3:4, :]).astype(

time: 423 us -> 392 us (0.927)
  waiting for transfers between devices: 367 us -> 332 us
  blocking collectives: 0 us -> 6.92 us
    psum x1 -> x0, waiting for transfers between devices: 34.3 us -> none  [body(): lax.psum(partial_value.astype(jnp.bfloat16), 'hid').astype(jnp.float32)]
    all_gather x0 -> x1, blocking collectives: none -> 6.92 us  [body(): lax.all_gather(partial_value.astype(jnp.bfloat16), 'hid')]
  transfers between devices with their start and end apart: 4 -> 3, of which waited for: 4 -> 3; matrix products, arithmetic and copies ran while one was open for 3% -> 3% of each run, Pallas kernels for 0% -> 0%
where the time goes in v1:
time: 392 us; the launch traced here: 391 us
  waiting for transfers between devices  332 us (85%)
  local copies, waits for them, and re-layouts  21.5 us (5%)
  between operations  14.8 us (4%)
  matrix products  12.7 us (3%)
  blocking collectives  6.92 us (2%)
    all_gather x1, waiting for transfers between devices, body(): lax.all_gather(qkv_weight, ('item', 'rows'), axis=1, tiled=True)  137 us
    all_gather x1, waiting for transfers between devices, body(): lax.all_gather(out_weight, ('item', 'rows'), axis=1, tiled=True)  109 us
    all_gather x1, waiting for transfers between devices, body(): gathered = lax.all_gather(image_kv, 'rows', axis=2, tiled=True)  85.4 us
  transfers between devices with their start and end apart: 3, of which 3 were waited for; matrix products, arithmetic and copies ran while one was open for 3% of the time, Pallas kernels for 0%

profile of v1, /device:TPU:1, one launch (start us, length us, event | category | flops | bytes accessed | tf_op | source)
XLA Modules:
  0.0 391.4 jit_solution(8724827226614394941)
XLA Ops:
  7.2 0.0 all-gather.6.cloned.1.call-start
  7.2 1.4 copy.35
  8.6 0.0 all-gather.6.cloned.1.call-update
  8.6 0.0 all-gather.10.cloned.1.call-start
  8.7 0.7 all-gather.10.cloned.1.call-update
  9.4 0.0 all-gather.8.cloned.1.call-start
  9.5 0.1 fusion.51
  9.5 0.2 fusion.44
  9.8 0.8 convert_reduce_fusion
  10.6 0.1 convert_element_type.54
  10.7 1.2 fusion.58
  11.9 0.2 multiply_reduce_fusion.1
  12.1 0.3 fusion.25
  12.4 0.1 add_convert_fusion.1
  12.6 136.8 %all-gather.6.cloned.1.call-done = bf16[3,1536,384]{2,0,1:T(4,128)(2,1)} async-done(((bf16[3,6,384]{2,0,1:T(4,128)(2,1)}), bf16[3,1536,384]{2,0,1:T(4,128)(2,1)}) %all-gather.6.cloned.1.call-update) | async-done | bytes 3538960 | tf_op jit(solution)/shard_map/all_gather | solution.py:81
  149.4 3.1 fusion.20
  152.5 0.6 slice.48
  153.1 0.0 all-gather.8.cloned.1.call-update
  153.9 0.1 broadcast_and_fusion.1
  153.9 0.1 broadcast_and_fusion
  154.0 0.1 and.40
  154.1 0.7 fusion.56
  154.8 0.5 copy.37
  155.3 0.5 copy.39
  155.9 109.1 %all-gather.10.cloned.1.call-done = bf16[256,6,384]{2,1,0:T(8,128)(2,1)} async-done(((bf16[1,6,384]{2,1,0:T(8,128)(2,1)}), bf16[256,6,384]{2,1,0:T(8,128)(2,1)}) %all-gather.10.cloned.1.call-update) | async-done | bytes 1179664 | tf_op jit(solution)/shard_map/all_gather | solution.py:138
  265.0 3.3 reshape.277
  268.3 0.1 reshape_squeeze.15
  268.4 0.3 fusion.59
  268.7 0.2 fusion.29
  268.9 85.4 %all-gather.8.cloned.1.call-done = bf16[2,2,32,32,384]{4,3,2,1,0:T(8,128)(2,1)} async-done(((bf16[2,2,1,32,384]{4,3,2,1,0:T(8,128)(2,1)}), bf16[2,2,32,32,384]{4,3,2,1,0:T(8,128)(2,1)}) %all-gather.8.cloned.1.call-update) | async-done | bytes 3145744 | tf_op jit(solution)/shard_map/all_gather | solution.py:104
  354.4 3.5 fusion.55
  357.8 3.7 reshape_squeeze.18
  361.6 3.4 fusion.60
  365.0 5.9 %reshape_squeeze.19 = bf16[2,1024,6,64]{3,2,1,0:T(8,128)(2,1)} reshape(bf16[1,2,32,32,384]{4,3,2,1,0:T(8,128)(2,1)} %get-tuple-element.5) | data formatting | bytes 3145728 | tf_op jit(solution)/shard_map/reshape;squeeze | solution.py:110
  370.9 0.4 fusion.8
  371.3 3.3 fusion.16
  374.6 0.3 fusion.19
  375.0 0.1 convert_element_type.62
  375.1 0.7 copy-done.1
  375.9 0.5 convolution_convert_fusion
  376.4 6.9 %all-gather = bf16[128,1536]{1,0:T(8,128)(2,1)S(1)} all-gather(bf16[64,1536]{1,0:T(8,128)(2,1)S(1)} %convolution_convert_fusion), channel_id=2, replica_groups=mesh['item'=8,'rows'=32,'hid'=2] {'hid'}, dimensions={0}, use_global_device_ids=true | all-gather | bytes 589824 | tf_op jit(solution)/shard_map/all_gather | solution.py:141
  383.3 0.1 reduce_sum.76
  383.4 0.1 fusion.40
  383.5 0.2 multiply_reduce_fusion
  383.7 0.3 broadcast_multiply_fusion
  384.0 0.1 mul.213
  384.1 0.1 mul.214
  384.2 0.6 fusion.57
  (30 shorter events, 0.2 us)
Async XLA Ops:
  7.2 4.9 %copy-start = (f32[16,5,1536]{2,0,1:T(8,128)S(1)}, f32[16,5,1536]{2,0,1:T(8,128)}, u32[]{:S(2)}) copy-start(f32[16,5,1536]{2,0,1:T(8,128)} %param.16) | copy-start | bytes 1474564
  7.2 4.9 %copy-start.4 = (s32[2]{0:T(128)S(1)}, s32[2]{0:T(128)}, u32[]{:S(2)}) copy-start(s32[2]{0:T(128)} %param.14) | copy-start | bytes 28
  7.2 142.2 %all-gather.6.cloned.1.call-start = ((), (), s32[]{:S(2)}) async-start(), calls=%async_computation | async-start | bytes 4737024 | tf_op jit(solution)/shard_map/all_gather | solution.py:81
  8.6 256.3 %all-gather.10.cloned.1.call-start = ((), (), s32[]{:S(2)}) async-start(), calls=%async_computation.2 | async-start | bytes 1579008 | tf_op jit(solution)/shard_map/all_gather | solution.py:138
  9.4 345.0 %all-gather.8.cloned.1.call-start = ((), (), s32[]{:S(2)}) async-start(), calls=%async_computation.1 | async-start | bytes 3244032 | tf_op jit(solution)/shard_map/all_gather | solution.py:104
  149.4 4.5 %copy-start.5 = (s32[2]{0:T(128)S(1)}, s32[2]{0:T(128)}, u32[]{:S(2)}) copy-start(s32[2]{0:T(128)} %param.12) | copy-start | bytes 28
  149.4 4.5 %copy-start.6 = (s32[2]{0:T(128)S(1)}, s32[2]{0:T(128)}, u32[]{:S(2)}) copy-start(s32[2]{0:T(128)} %param.13) | copy-start | bytes 28
  149.4 4.7 %copy-start.2 = (bf16[2,2,154,384]{3,1,2,0:T(2,128)(2,1)S(1)}, bf16[2,2,154,384]{3,1,2,0:T(2,128)(2,1)}, u32[]{:S(2)}) copy-start(bf16[2,2,154,384]{3,1,2,0:T(2,128)(2,1)} %param.17) | copy-start | bytes 1419268
  374.6 1.3 copy-start.1
  375.9 7.9 %copy-start.7 = (bf16[1536,64]{0,1:T(8,128)(2,1)S(1)}, bf16[1536,64]{0,1:T(8,128)(2,1)}, u32[]{:S(2)}) copy-start(bf16[1536,64]{0,1:T(8,128)(2,1)} %param.21) | copy-start | bytes 589828
  383.3 0.9 copy-start.3
Sparse Core Ops, SparseCore 0:
  12.5 136.7 all-gather.5
  153.5 111.3 all-gather.9
  268.3 86.0 all-gather.7
